TPU v7x, 32 devices: a whole 2x2x4 slice. The times are simulated.
32 devices in a mesh: layer: 2 (over core), feat: 4 (over y, x), seq: 4 (over z).
Axes of the slice: x: 2, y: 2, z: 4, core: 2. Of those that a mesh axis runs over, the one named last changes fastest.
Arguments:
- mlp_inputs: bfloat16 [2, 768, 2304], P('layer', 'seq'), may hold values from -6 to 6
- enc_weight: bfloat16 [2, 2304, 4096], P('layer', 'seq', 'feat'), may hold values from -0.125 to 0.125
- enc_bias: float32 [2, 4096], P('layer', 'feat'), may hold values from -3 to 3
- dec_weight: bfloat16 [2, 4096, 2304], P('layer', 'feat', 'seq'), may hold values from -0.1875 to 0.1875
- dec_cross: bfloat16 [4096, 2304], P('feat', ('layer', 'seq')), may hold values from -0.1875 to 0.1875
- dec_bias: float32 [2, 2304], P('layer', 'feat'), may hold values from -3 to 3
Outputs:
- recon: bfloat16 [2, 768, 2304], P('layer', 'seq', 'feat')
All inputs are finite; a program needn't handle non-finite values.
Results may differ from a plain program's by a relative error of at most 0.0047.
Values may be sent and summed in bfloat16 or wider, within the bound.
A program may use at most 64 MiB of HBM per device.

v0:
```python
import jax
import jax.numpy as jnp
from jax import lax
from jax.sharding import PartitionSpec as P


def passed_along(x, axis, by):
    devices = lax.axis_size(axis)
    pairs = [(i, i + by) for i in range(devices) if 0 <= i + by < devices]
    return lax.ppermute(x, axis, pairs)


def per_device(mlp_inputs, enc_weight, enc_bias, dec_weight, dec_cross, dec_bias):
    token_rows = mlp_inputs[0]
    layer_index = lax.axis_index("layer")
    pre_acts = jnp.dot(
        token_rows,
        lax.all_gather(enc_weight[0], "seq", axis=0, tiled=True),
        preferred_element_type=jnp.float32,
    )
    features = jnp.maximum(pre_acts + enc_bias[0], 0.0).astype(jnp.bfloat16)
    own_terms = jnp.dot(
        features,
        lax.all_gather(dec_weight[0], "seq", axis=1, tiled=True),
        preferred_element_type=jnp.float32,
    )
    half_rows = features.shape[0] // 2
    sent_half = passed_along(features[half_rows:], "layer", 1)
    cross_input = jnp.where(layer_index == 0, features[:half_rows], sent_half)
    cross_terms = jnp.dot(
        cross_input,
        lax.all_gather(dec_cross, ("layer", "seq"), axis=1, tiled=True),
        preferred_element_type=jnp.float32,
    )
    own_sums, cross_sums = (
        lax.psum_scatter(own_terms, "feat", scatter_dimension=1, tiled=True),
        lax.psum_scatter(cross_terms, "feat", scatter_dimension=1, tiled=True),
    )
    moved_sums = passed_along(cross_sums, "layer", 1)
    cross_full = jnp.concatenate([moved_sums, cross_sums], axis=0)
    total = own_sums + dec_bias[0] + jnp.where(layer_index == 1, cross_full, 0.0)
    return total.astype(jnp.bfloat16)[None]


def solution(mesh):
    placed = (
        P("layer", "seq", None),
        P("layer", "seq", "feat"),
        P("layer", "feat"),
        P("layer", "feat", "seq"),
        P("feat", ("layer", "seq")),
        P("layer", "feat"),
    )
    return jax.shard_map(
        per_device, mesh=mesh, in_specs=placed, out_specs=P("layer", "seq", "feat"), check_vma=False
    )
```

profile of v0, /device:TPU:0, one launch (start us, length us, event | category | flops | bytes accessed | tf_op | source)
XLA Modules:
  0.0 320.9 jit_solution(13372327382899990657)
XLA Ops:
  6.5 0.0 copy-start
  6.5 0.0 all-gather.8.cloned.1.call-start
  6.5 0.7 all-gather.8.cloned.1.call-update
  7.3 0.0 all-gather.6.cloned.1.call-start
  7.3 0.7 all-gather.6.cloned.1.call-update
  8.0 0.0 all-gather.10.cloned.1.call-start
  8.1 0.7 all-gather.10.cloned.1.call-update
  8.7 0.0 reduce-scatter.9.cloned.1.call-start
  8.8 92.3 %all-gather.8.cloned.1.call-done = bf16[1,2304,1024]{2,1,0:T(8,128)(2,1)} async-done(((bf16[1,576,1024]{2,1,0:T(8,128)(2,1)}), bf16[1,2304,1024]{2,1,0:T(8,128)(2,1)}) %all-gather.8.cloned.1.call-update) | async-done | bytes 4718608 | tf_op jit(solution)/shard_map/all_gather | solution.py:18
  101.0 0.0 copy-done
  101.0 3.4 %fusion.13 = bf16[192,1024]{1,0:T(8,128)(2,1)S(1)} fusion(bf16[1,2304,1024]{2,1,0:T(8,128)(2,1)} %all-gather.8.cloned.1.call-done, bf16[1,192,2304]{2,1,0:T(8,128)(2,1)S(1)} %copy-done, f32[1024]{0:T(1024)} %bitcast.30), kind=kOutput, calls=%fused_computation.8 | convolution fusion | flops 906559488 | bytes 6000640 | tf_op jit(solution)/shard_map/dot_general | solution.py:16
  104.5 1.7 collective-permute-start
  106.2 1.0 collective-permute-done
  107.2 45.0 %all-gather.6.cloned.1.call-done = bf16[1024,2304]{0,1:T(8,128)(2,1)} async-done(((bf16[1024,288]{0,1:T(8,128)(2,1)}), bf16[1024,2304]{0,1:T(8,128)(2,1)}) %all-gather.6.cloned.1.call-update) | async-done | bytes 4718608 | tf_op jit(solution)/shard_map/all_gather | solution.py:32
  152.3 4.7 %convolution_bitcast_fusion = f32[2304,96]{1,0:T(8,128)} fusion(bf16[1024,2304]{0,1:T(8,128)(2,1)} %all-gather.6.cloned.1.call-done, bf16[96,1024]{1,0:T(8,128)(2,1)S(1)} %collective-permute-done, bf16[192,1024]{1,0:T(8,128)(2,1)S(1)} %fusion.13, pred[]{:T(512)S(6)} %eq.7), kind=kOutput, calls=%fused_computation.5 | convolution fusion | flops 453083136 | bytes 5996545
  157.0 0.0 reduce-scatter.9.cloned.1.call-update
  157.1 0.0 copy-start.1
  157.1 0.0 reduce-scatter.7.cloned.1.call-start
  157.1 84.9 %all-gather.10.cloned.1.call-done = bf16[1,1024,2304]{1,2,0:T(8,128)(2,1)} async-done(((bf16[1,1024,576]{1,2,0:T(8,128)(2,1)}), bf16[1,1024,2304]{1,2,0:T(8,128)(2,1)}) %all-gather.10.cloned.1.call-update) | async-done | bytes 4718608 | tf_op jit(solution)/shard_map/all_gather | solution.py:24
  242.0 5.2 %fusion.4 = f32[2304,192]{1,0:T(8,128)} fusion(bf16[192,1024]{1,0:T(8,128)(2,1)S(1)} %fusion.13, bf16[1,1024,2304]{1,2,0:T(8,128)(2,1)} %all-gather.10.cloned.1.call-done), kind=kOutput, calls=%fused_computation.4 | convolution fusion | flops 905969664 | bytes 6881280
  247.2 0.0 reduce-scatter.7.cloned.1.call-update
  247.2 24.7 %reduce-scatter.9.cloned.1.call-done = f32[576,96]{1,0:T(8,128)} async-done(((f32[2304,96]{1,0:T(8,128)}), f32[576,96]{1,0:T(8,128)}) %reduce-scatter.9.cloned.1.call-update) | async-done | bytes 221200
  272.0 1.1 copy.10
  273.1 1.6 collective-permute-start.1
  274.7 0.0 copy-done.1
  274.7 37.5 %reduce-scatter.7.cloned.1.call-done = f32[576,192]{1,0:T(8,128)} async-done(((f32[2304,192]{1,0:T(8,128)}), f32[576,192]{1,0:T(8,128)}) %reduce-scatter.7.cloned.1.call-update) | async-done | bytes 442384
  312.3 1.3 copy.8
  313.6 0.0 collective-permute-done.1
  313.6 0.8 fusion.19
  (2 shorter events, 0.0 us)
Async XLA Ops:
  6.5 94.5 %copy-start = (bf16[1,192,2304]{2,1,0:T(8,128)(2,1)S(1)}, bf16[1,192,2304]{2,1,0:T(8,128)(2,1)}, u32[]{:S(2)}) copy-start(bf16[1,192,2304]{2,1,0:T(8,128)(2,1)} %param.6) | copy-start | bytes 2654212
  6.5 94.5 %all-gather.8.cloned.1.call-start = ((), (), s32[]{:S(2)}) async-start(), calls=%async_computation.3 | async-start | bytes 5898240 | tf_op jit(solution)/shard_map/all_gather | solution.py:18
  7.3 145.0 %all-gather.6.cloned.1.call-start = ((), (), s32[]{:S(2)}) async-start(), calls=%async_computation.2 | async-start | bytes 5308416 | tf_op jit(solution)/shard_map/all_gather | solution.py:32
  8.0 234.0 %all-gather.10.cloned.1.call-start = ((), (), s32[]{:S(2)}) async-start(), calls=%async_computation.4 | async-start | bytes 5898240 | tf_op jit(solution)/shard_map/all_gather | solution.py:24
  8.7 263.2 %reduce-scatter.9.cloned.1.call-start = ((), (), s32[]{:S(2)}) async-start(), calls=%async_computation.6 | async-start | bytes 1474560
  104.5 2.7 collective-permute-start
  157.1 117.6 %copy-start.1 = (f32[1,576]{1,0:T(1,128)S(1)}, f32[1,576]{1,0:T(1,128)}, u32[]{:S(2)}) copy-start(f32[1,576]{1,0:T(1,128)} %param.11) | copy-start | bytes 6916
  157.1 155.2 %reduce-scatter.7.cloned.1.call-start = ((), (), s32[]{:S(2)}) async-start(), calls=%async_computation.5 | async-start | bytes 2949120
  273.1 40.5 %collective-permute-start.1 = (f32[96,576]{1,0:T(8,128)S(1)}, f32[96,576]{1,0:T(8,128)S(1)}, u32[]{:S(2)}, u32[]{:S(2)}) collective-permute-start(f32[96,576]{1,0:T(8,128)S(1)} %copy.10), channel_id=1, source_target_pairs={{0,16},{1,17},{2,18},{3,19},{4,20},{5,21},{6,22},{7,23},{8,24},{9,... | collective-permute-start | bytes 663560 | tf_op jit(solution)/shard_map/ppermute | solution.py:10
Sparse Core Ops, SparseCore 0:
  8.9 92.0 all-gather.7
  102.6 49.6 all-gather.5
  153.9 88.1 all-gather.9
  244.8 27.1 reduce-scatter.8
  274.9 37.3 reduce-scatter.6
where the time goes:
time: 321 us
  waiting for transfers between devices  288 us (90%)
  matrix products  13.3 us (4%)
  between operations  13.2 us (4%)
  starting transfers between devices  3.46 us (1%)
    all_gather x1, waiting for transfers between devices, per_device(): lax.all_gather(enc_weight[0], 'seq', axis=0, tiled=True)  92.3 us
    all_gather x1, waiting for transfers between devices, per_device(): lax.all_gather(dec_weight[0], 'seq', axis=1, tiled=True)  84.9 us
    unnamed x7, waiting for transfers between devices  64.4 us
    all_gather x1, waiting for transfers between devices, per_device(): lax.all_gather(dec_cross, ('layer', 'seq'), axis=1, tiled=True)  45 us
    unnamed x2, matrix products  9.92 us
  transfers between devices with their start and end apart: 7, of which 6 were waited for; matrix products, arithmetic and copies ran while one was open for 5% of the time, Pallas kernels for 0%

commit v1 on v0

--- a/solution.py
+++ b/solution.py
@@ -2,6 +2,22 @@
 import jax.numpy as jnp
 from jax import lax
 from jax.sharding import PartitionSpec as P
+
+
+def gather_around(x, axis, dim):
+    ways, here, step = (lax.axis_size(axis), lax.axis_index(axis), x.shape[dim])
+    lengths = [n * ways if d == dim else n for d, n in enumerate(x.shape)]
+    full = lax.dynamic_update_slice_in_dim(jnp.zeros(lengths, x.dtype), x, here * step, axis=dim)
+    going_up = going_down = x
+    for far in range(1, ways // 2 + 1):
+        going_up = lax.ppermute(going_up, axis, [(d, (d + 1) % ways) for d in range(ways)])
+        full = lax.dynamic_update_slice_in_dim(full, going_up, (here - far) % ways * step, axis=dim)
+        if 2 * far < ways:
+            going_down = lax.ppermute(going_down, axis, [(d, (d - 1) % ways) for d in range(ways)])
+            full = lax.dynamic_update_slice_in_dim(
+                full, going_down, (here + far) % ways * step, axis=dim
+            )
+    return full
 
 
 def passed_along(x, axis, by):
@@ -14,9 +30,7 @@
     token_rows = mlp_inputs[0]
     layer_index = lax.axis_index("layer")
     pre_acts = jnp.dot(
-        token_rows,
-        lax.all_gather(enc_weight[0], "seq", axis=0, tiled=True),
-        preferred_element_type=jnp.float32,
+        token_rows, gather_around(enc_weight[0], "seq", 0), preferred_element_type=jnp.float32
     )
     features = jnp.maximum(pre_acts + enc_bias[0], 0.0).astype(jnp.bfloat16)
     own_terms = jnp.dot(

time: 321 us -> 285 us (0.89)
  waiting for transfers between devices: 288 us -> 206 us
  starting transfers between devices: 3.46 us -> 46.7 us
  local copies, waits for them, and re-layouts: 2.41 us -> 6.03 us
    all_gather x1 -> x0, waiting for transfers between devices: 92.3 us -> none  [per_device(): lax.all_gather(enc_weight[0], 'seq', axis=0, tiled=True)]
    ppermute x0 -> x3, waiting for transfers between devices: none -> 82.4 us  [the longest x2 75.9 us: gather_around(): lax.ppermute(going_up, axis, [(d, (d + 1) % ways) for d in range(ways)])]
    all_gather x1, waiting for transfers between devices: 45 us -> 0.01 us  [per_device(): lax.all_gather(dec_cross, ('layer', 'seq'), axis=1, tiled=True)]
    ppermute x0 -> x3, starting transfers between devices: none -> 43.7 us  [the longest x2 41.6 us: gather_around(): lax.ppermute(going_up, axis, [(d, (d + 1) % ways) for d in range(ways)])]
    all_gather x1, waiting for transfers between devices: 84.9 us -> 58.4 us  [per_device(): lax.all_gather(dec_weight[0], 'seq', axis=1, tiled=True)]
    unnamed x7 -> x6, waiting for transfers between devices: 64.4 us -> 64.6 us
  transfers between devices with their start and end apart: 7 -> 9, of which waited for: 6 -> 7; matrix products, arithmetic and copies ran while one was open for 5% -> 6% of each run, Pallas kernels for 0% -> 0%
where the time goes in v1:
time: 285 us; the launch traced here: 284 us
  waiting for transfers between devices  206 us (72%)
  starting transfers between devices  46.7 us (16%)
  between operations  13.3 us (5%)
  matrix products  11.1 us (4%)
  local copies, waits for them, and re-layouts  6.03 us (2%)
    ppermute x2, waiting for transfers between devices, gather_around(): lax.ppermute(going_up, axis, [(d, (d + 1) % ways) for d in range(ways)])  75.9 us
    unnamed x6, waiting for transfers between devices  64.6 us
    all_gather x1, waiting for transfers between devices, per_device(): lax.all_gather(dec_weight[0], 'seq', axis=1, tiled=True)  58.4 us
    ppermute x2, starting transfers between devices, gather_around(): lax.ppermute(going_up, axis, [(d, (d + 1) % ways) for d in range(ways)])  41.6 us
    unnamed x2, matrix products  9.99 us
    ppermute x1, waiting for transfers between devices, gather_around(): lax.ppermute(going_down, axis, [(d, (d - 1) % ways) for d in range(ways)])  6.52 us
  transfers between devices with their start and end apart: 9, of which 7 were waited for; matrix products, arithmetic and copies ran while one was open for 6% of the time, Pallas kernels for 0%

profile of v1, /device:TPU:0, one launch (start us, length us, event | category | flops | bytes accessed | tf_op | source)
XLA Modules:
  0.0 284.2 jit_solution(3915319443135844136)
XLA Ops:
  6.5 0.7 all-gather.4.cloned.1.call-update
  7.3 0.0 all-gather.6.cloned.1.call-start
  7.3 0.7 all-gather.6.cloned.1.call-update
  8.0 0.0 reduce-scatter.9.cloned.1.call-start
  8.1 3.1 %collective-permute-start = (bf16[576,1024]{1,0:T(8,128)(2,1)}, bf16[576,1024]{1,0:T(8,128)(2,1)S(1)}, u32[]{:S(2)}, u32[]{:S(2)}) collective-permute-start(bf16[576,1024]{1,0:T(8,128)(2,1)} %bitcast.23), channel_id=1, source_target_pairs={{0,1},{1,2},{2,3},{3,0},{4,5},{5,6},{6,7},{7,4},{8,9},{9,10},{10,1... | collective-permute-start | bytes 3538952 | tf_op jit(solution)/shard_map/ppermute | solution.py:13
  11.2 2.1 collective-permute-start.1
  13.3 43.2 %collective-permute-done = bf16[576,1024]{1,0:T(8,128)(2,1)S(1)} collective-permute-done((bf16[576,1024]{1,0:T(8,128)(2,1)}, bf16[576,1024]{1,0:T(8,128)(2,1)S(1)}, u32[]{:S(2)}, u32[]{:S(2)}) %collective-permute-start) | collective-permute-done | bytes 1179680 | tf_op jit(solution)/shard_map/ppermute | solution.py:13
  56.5 38.5 %collective-permute-start.2 = (bf16[576,1024]{1,0:T(8,128)(2,1)S(1)}, bf16[576,1024]{1,0:T(8,128)(2,1)}, u32[]{:S(2)}, u32[]{:S(2)}) collective-permute-start(bf16[576,1024]{1,0:T(8,128)(2,1)S(1)} %collective-permute-done), channel_id=1, source_target_pairs={{0,1},{1,2},{2,3},{3,0},{4,5},{5,6},{6,7},{7,4},{8,9},{9,10},{10,1... | collective-permute-start | bytes 3538952 | tf_op jit(solution)/shard_map/ppermute | solution.py:13
  94.9 0.6 broadcast_in_dim.10
  95.6 0.0 copy-start.3
  95.6 0.1 constant_dynamic-update-slice_fusion.3
  95.7 0.1 constant_dynamic-update-slice_fusion.2
  95.8 6.5 %collective-permute-done.1 = bf16[576,1024]{1,0:T(8,128)(2,1)} collective-permute-done((bf16[576,1024]{1,0:T(8,128)(2,1)}, bf16[576,1024]{1,0:T(8,128)(2,1)}, u32[]{:S(2)}, u32[]{:S(2)}) %collective-permute-start.1) | collective-permute-done | bytes 1179680 | tf_op jit(solution)/shard_map/ppermute | solution.py:16
  102.3 1.4 constant_dynamic-update-slice_fusion.1
  103.7 32.6 %collective-permute-done.2 = bf16[576,1024]{1,0:T(8,128)(2,1)} collective-permute-done((bf16[576,1024]{1,0:T(8,128)(2,1)S(1)}, bf16[576,1024]{1,0:T(8,128)(2,1)}, u32[]{:S(2)}, u32[]{:S(2)}) %collective-permute-start.2) | collective-permute-done | bytes 1179680 | tf_op jit(solution)/shard_map/ppermute | solution.py:13
  136.4 1.4 constant_dynamic-update-slice_fusion
  137.8 1.1 fusion.6
  138.9 1.3 collective-permute-start.3
  140.2 1.0 collective-permute-done.3
  141.3 4.8 %convolution_bitcast_fusion = f32[2304,96]{1,0:T(8,128)} fusion(bf16[1024,2304]{0,1:T(8,128)(2,1)} %all-gather.4.cloned.1.call-done, bf16[96,1024]{1,0:T(8,128)(2,1)S(1)} %collective-permute-done.3, bf16[192,1024]{1,0:T(8,128)(2,1)S(1)} %bitcast.26, pred[]{:T(512)S(6)} %eq.11), kind=kOutput, calls=%fused_computation.3 | convolution fusion | flops 453083136 | bytes 5996545
  146.1 0.0 reduce-scatter.9.cloned.1.call-update
  146.1 0.0 copy-start.2
  146.1 0.0 reduce-scatter.7.cloned.1.call-start
  146.2 58.4 %all-gather.6.cloned.1.call-done = bf16[1,1024,2304]{1,2,0:T(8,128)(2,1)} async-done(((bf16[1,1024,576]{1,2,0:T(8,128)(2,1)}), bf16[1,1024,2304]{1,2,0:T(8,128)(2,1)}) %all-gather.6.cloned.1.call-update) | async-done | bytes 4718608 | tf_op jit(solution)/shard_map/all_gather | solution.py:38
  204.6 5.2 %fusion.2 = f32[2304,192]{1,0:T(8,128)} fusion(bf16[1024,192]{0,1:T(8,128)(2,1)S(1)} %fusion.6, bf16[1,1024,2304]{1,2,0:T(8,128)(2,1)} %all-gather.6.cloned.1.call-done), kind=kOutput, calls=%fused_computation.2 | convolution fusion | flops 905969664 | bytes 6881280
  209.7 0.0 reduce-scatter.7.cloned.1.call-update
  209.8 25.6 %reduce-scatter.9.cloned.1.call-done = f32[576,96]{1,0:T(8,128)} async-done(((f32[2304,96]{1,0:T(8,128)}), f32[576,96]{1,0:T(8,128)}) %reduce-scatter.9.cloned.1.call-update) | async-done | bytes 221200
  235.3 1.1 copy.10
  236.4 1.6 collective-permute-start.4
  238.1 37.6 %reduce-scatter.7.cloned.1.call-done = f32[576,192]{1,0:T(8,128)} async-done(((f32[2304,192]{1,0:T(8,128)}), f32[576,192]{1,0:T(8,128)}) %reduce-scatter.7.cloned.1.call-update) | async-done | bytes 442384
  275.6 1.3 copy.8
  276.9 0.8 fusion.10
  (11 shorter events, 0.0 us)
Async XLA Ops:
  6.5 131.2 %copy-start = (bf16[1,192,2304]{2,1,0:T(8,128)(2,1)S(1)}, bf16[1,192,2304]{2,1,0:T(8,128)(2,1)}, u32[]{:S(2)}) copy-start(bf16[1,192,2304]{2,1,0:T(8,128)(2,1)} %param.6) | copy-start | bytes 2654212
  6.5 89.0 %copy-start.1 = (bf16[1,576,1024]{2,1,0:T(8,128)(2,1)S(1)}, bf16[1,576,1024]{2,1,0:T(8,128)(2,1)}, u32[]{:S(2)}) copy-start(bf16[1,576,1024]{2,1,0:T(8,128)(2,1)} %param.7) | copy-start | bytes 3538948
  6.5 134.7 %all-gather.4.cloned.1.call-start = ((), (), s32[]{:S(2)}) async-start(), calls=%async_computation.2 | async-start | bytes 5308416 | tf_op jit(solution)/shard_map/all_gather | solution.py:46
  7.3 197.3 %all-gather.6.cloned.1.call-start = ((), (), s32[]{:S(2)}) async-start(), calls=%async_computation.3 | async-start | bytes 5898240 | tf_op jit(solution)/shard_map/all_gather | solution.py:38
  8.0 227.3 %reduce-scatter.9.cloned.1.call-start = ((), (), s32[]{:S(2)}) async-start(), calls=%async_computation.5 | async-start | bytes 1474560
  8.1 48.4 %collective-permute-start = (bf16[576,1024]{1,0:T(8,128)(2,1)}, bf16[576,1024]{1,0:T(8,128)(2,1)S(1)}, u32[]{:S(2)}, u32[]{:S(2)}) collective-permute-start(bf16[576,1024]{1,0:T(8,128)(2,1)} %bitcast.23), channel_id=1, source_target_pairs={{0,1},{1,2},{2,3},{3,0},{4,5},{5,6},{6,7},{7,4},{8,9},{9,10},{10,1... | collective-permute-start | bytes 3538952 | tf_op jit(solution)/shard_map/ppermute | solution.py:13
  11.2 91.2 %collective-permute-start.1 = (bf16[576,1024]{1,0:T(8,128)(2,1)}, bf16[576,1024]{1,0:T(8,128)(2,1)}, u32[]{:S(2)}, u32[]{:S(2)}) collective-permute-start(bf16[576,1024]{1,0:T(8,128)(2,1)} %bitcast.24), channel_id=1, source_target_pairs={{0,3},{1,0},{2,1},{3,2},{4,7},{5,4},{6,5},{7,6},{8,11},{9,8},{10,9... | collective-permute-start | bytes 3538952 | tf_op jit(solution)/shard_map/ppermute | solution.py:16
  56.5 79.9 %collective-permute-start.2 = (bf16[576,1024]{1,0:T(8,128)(2,1)S(1)}, bf16[576,1024]{1,0:T(8,128)(2,1)}, u32[]{:S(2)}, u32[]{:S(2)}) collective-permute-start(bf16[576,1024]{1,0:T(8,128)(2,1)S(1)} %collective-permute-done), channel_id=1, source_target_pairs={{0,1},{1,2},{2,3},{3,0},{4,5},{5,6},{6,7},{7,4},{8,9},{9,10},{10,1... | collective-permute-start | bytes 3538952 | tf_op jit(solution)/shard_map/ppermute | solution.py:13
  95.6 42.2 %copy-start.3 = (f32[1,1024]{1,0:T(1,128)S(1)}, f32[1,1024]{1,0:T(1,128)}, u32[]{:S(2)}) copy-start(f32[1,1024]{1,0:T(1,128)} %param.8) | copy-start | bytes 12292
  138.9 2.4 collective-permute-start.3
  146.1 91.9 %copy-start.2 = (f32[1,576]{1,0:T(1,128)S(1)}, f32[1,576]{1,0:T(1,128)}, u32[]{:S(2)}) copy-start(f32[1,576]{1,0:T(1,128)} %param.11) | copy-start | bytes 6916
  146.1 129.5 %reduce-scatter.7.cloned.1.call-start = ((), (), s32[]{:S(2)}) async-start(), calls=%async_computation.4 | async-start | bytes 2949120
  236.4 40.5 %collective-permute-start.4 = (f32[96,576]{1,0:T(8,128)S(1)}, f32[96,576]{1,0:T(8,128)S(1)}, u32[]{:S(2)}, u32[]{:S(2)}) collective-permute-start(f32[96,576]{1,0:T(8,128)S(1)} %copy.10), channel_id=1, source_target_pairs={{0,16},{1,17},{2,18},{3,19},{4,20},{5,21},{6,22},{7,23},{8,24},{9,... | collective-permute-start | bytes 663560 | tf_op jit(solution)/shard_map/ppermute | solution.py:26
Sparse Core Ops, SparseCore 0:
  8.9 89.0 all-gather.3
  99.6 104.9 all-gather.5
  207.5 27.8 reduce-scatter.8
  238.2 37.3 reduce-scatter.6
